TPU v7x, 256 devices: a whole 4x4x8 slice. The times are simulated.
256 devices in a mesh: cfg: 2 (over core), req: 8 (over z), tok: 16 (over y, x).
Axes of the slice: x: 4, y: 4, z: 8, core: 2. Of those that a mesh axis runs over, the one named last changes fastest.
Arguments:
- image_tokens: bfloat16 [2, 8, 1024, 2432], P('cfg', 'req', 'tok')
- text_tokens: bfloat16 [2, 8, 256, 2432], P('cfg', 'req', 'tok')
- text_lengths: int32 [2, 8], P('cfg', 'req'), may hold values from 1 to 256, as said below
- modulation: float32 [2, 8, 10, 2432], P('cfg', 'req'), may hold values from -3 to 3
- latent: float32 [8, 1024, 64], P('req', 'tok', 'cfg'), may hold values from -6 to 6
- guidance: float32 [8], P('req'), may hold values from 2 to 7
- step_index: int32 [8], P('req'), may hold values from 0 to 27
- qkv_weight: bfloat16 [2432, 3, 2048], P(None, None, 'tok'), may hold values from -0.125 to 0.125
- text_kv_weight: bfloat16 [2432, 2, 2048], P(None, None, 'tok'), may hold values from -0.125 to 0.125
- query_gain: float32 [64], replicated, may hold values from 1.2 to 2.4
- key_gain: float32 [64], replicated, may hold values from 1.2 to 2.4
- text_key_gain: float32 [64], replicated, may hold values from 1.2 to 2.4
- out_weight: bfloat16 [2048, 2432], P('tok'), may hold values from -0.125 to 0.125
- up_weight: bfloat16 [2432, 9728], P(None, 'tok'), may hold values from -0.125 to 0.125
- down_weight: bfloat16 [9728, 2432], P('tok'), may hold values from -0.0625 to 0.0625
- final_weight: bfloat16 [2432, 64], replicated, may hold values from -0.125 to 0.125
Outputs:
- velocity: float32 [8, 1024, 64], P('req', 'tok', 'cfg')
- next_latent: float32 [8, 1024, 64], P('req', 'tok', 'cfg')
Inputs may be any that keep to these rules, and one draw needn't show every extreme that they name: `text_lengths`: some half of some request has all 256 text slots live, and another has a single live one.
All inputs are finite; a program needn't handle non-finite values.
Results may differ from a plain program's by a relative error of at most 0.012.
Values may be sent and summed in bfloat16 or wider, within the bound.
No kernel may reach another device: no remote copies, remote signals or barrier semaphores. Data moves between devices by JAX's collectives and lax.ppermute only.
A program may use at most 128 MiB of HBM per device.

v0:
```python
import jax
import jax.numpy as jnp
from jax import lax
from jax.sharding import PartitionSpec as P

HEAD = 64
STEPS = 28
epsilon = 1e-06
shift_factor = 3.0


def swapped(value, axis, distance):
    mask = 2**distance
    pairs = [(source, source ^ mask) for source in range(lax.axis_size(axis))]
    return lax.ppermute(value, axis, pairs)


def layer_norm(values):
    row_mean = jnp.mean(values, axis=-1, keepdims=True)
    centered = values - row_mean
    variance = jnp.mean(centered * centered, axis=-1, keepdims=True)
    return centered * lax.rsqrt(variance + epsilon)


def modulate(values, shifts, shift_at, scale_at):
    return (layer_norm(values) * (1.0 + shifts[scale_at]) + shifts[shift_at]).astype(jnp.bfloat16)


def rms_heads(values, scaling):
    mean_square = jnp.mean(values * values, axis=-1, keepdims=True)
    return values * lax.rsqrt(mean_square + epsilon) * scaling


def sigma_of(step_value):
    moment = 1.0 - step_value.astype(jnp.float32) / STEPS
    return shift_factor * moment / (1.0 + (shift_factor - 1.0) * moment)


def gather_tokens(local_rows, project):
    return project(lax.all_gather(local_rows, "tok", axis=0, tiled=True), jnp.int32(0))


def scatter_tokens(term, own_count):
    return lax.psum_scatter(
        term(jnp.int32(0), own_count * lax.axis_size("tok")).astype(jnp.bfloat16),
        "tok",
        scatter_dimension=0,
        tiled=True,
    ).astype(jnp.float32)


def local(
    image_tokens,
    text_tokens,
    text_lengths,
    modulation,
    latent,
    guidance,
    step_index,
    qkv_weight,
    text_kv_weight,
    query_gain,
    key_gain,
    text_key_gain,
    out_weight,
    up_weight,
    down_weight,
    final_weight,
):
    shifts = modulation[0, 0]
    own_image = image_tokens[0, 0]
    own_text = text_tokens[0, 0]
    own_count = own_image.shape[0]
    feature_count = own_image.shape[1]
    head_cols = qkv_weight.shape[2]
    heads_local = head_cols // HEAD
    qkv_flat = qkv_weight.reshape(feature_count, 3 * head_cols)
    kv_flat = text_kv_weight.reshape(feature_count, 2 * head_cols)

    def project_image(portion, offset):
        row_total = portion.shape[0]
        mixed = jnp.dot(portion, qkv_flat, preferred_element_type=jnp.float32).reshape(
            row_total, 3, heads_local, HEAD
        )
        query = rms_heads(mixed[:, 0], query_gain)
        image_key = rms_heads(mixed[:, 1], key_gain)
        joined = jnp.concatenate([query, image_key, mixed[:, 2]], axis=1)
        return joined.reshape(row_total, 3 * head_cols).astype(jnp.bfloat16)

    def project_text(portion, offset):
        row_total = portion.shape[0]
        mixed = jnp.dot(portion, kv_flat, preferred_element_type=jnp.float32).reshape(
            row_total, 2, heads_local, HEAD
        )
        text_key = rms_heads(mixed[:, 0], text_key_gain)
        joined = jnp.concatenate([text_key, mixed[:, 1]], axis=1)
        return joined.reshape(row_total, 2 * head_cols).astype(jnp.bfloat16)

    def expand(portion, offset):
        return jax.nn.gelu(
            jnp.dot(portion, up_weight, preferred_element_type=jnp.float32), approximate=True
        ).astype(jnp.bfloat16)

    projected = gather_tokens(modulate(own_image.astype(jnp.float32), shifts, 0, 1), project_image)
    text_rows = gather_tokens(modulate(own_text.astype(jnp.float32), shifts, 6, 7), project_text)
    image_count = projected.shape[0]
    key_count = image_count + text_rows.shape[0]
    live_keys = lax.iota(jnp.int32, key_count) < image_count + text_lengths[0, 0]
    queries = projected[:, :head_cols]
    keys = jnp.concatenate(
        [projected[:, head_cols : 2 * head_cols], text_rows[:, :head_cols]], axis=0
    )
    values_all = jnp.concatenate([projected[:, 2 * head_cols :], text_rows[:, head_cols:]], axis=0)
    query_rows = min(image_count, 512)
    blocks = image_count // query_rows

    def one_task(task_index):
        head_index = task_index // blocks
        first_row = task_index % blocks * query_rows
        query_block = lax.dynamic_slice(queries, (first_row, head_index * HEAD), (query_rows, HEAD))
        key_head = lax.dynamic_slice_in_dim(keys, head_index * HEAD, HEAD, 1)
        value_head = lax.dynamic_slice_in_dim(values_all, head_index * HEAD, HEAD, 1)
        scores = jnp.dot(query_block, key_head.T, preferred_element_type=jnp.float32) * HEAD ** (
            -0.5
        )
        weights = jnp.where(live_keys[None, :], jnp.exp(scores), 0.0)
        probabilities = (weights / jnp.sum(weights, axis=1, keepdims=True)).astype(jnp.bfloat16)
        return jnp.dot(probabilities, value_head, preferred_element_type=jnp.float32).astype(
            jnp.bfloat16
        )

    outputs = lax.map(one_task, lax.iota(jnp.int32, heads_local * blocks))
    attention = (
        outputs.reshape(heads_local, image_count, HEAD)
        .transpose(1, 0, 2)
        .reshape(image_count, head_cols)
    )

    def attention_term(start_row, row_total):
        return jnp.dot(attention, out_weight, preferred_element_type=jnp.float32)

    residual = own_image.astype(jnp.float32) + shifts[2] * scatter_tokens(attention_term, own_count)
    hidden = gather_tokens(modulate(residual, shifts, 3, 4), expand)

    def mlp_term(start_row, row_total):
        return jnp.dot(hidden, down_weight, preferred_element_type=jnp.float32)

    second_sum = residual + shifts[5] * scatter_tokens(mlp_term, own_count)
    final_in = modulate(second_sum, shifts, 8, 9)
    prediction = jnp.dot(final_in, final_weight, preferred_element_type=jnp.float32)
    channel_half = prediction.shape[1] // 2
    half_index = lax.axis_index("cfg")
    kept = lax.dynamic_slice_in_dim(prediction, half_index * channel_half, channel_half, 1)
    given = lax.dynamic_slice_in_dim(prediction, (1 - half_index) * channel_half, channel_half, 1)
    partner = swapped(given, "cfg", 0)
    first_half = half_index == 0
    cond = jnp.where(first_half, kept, partner)
    uncond = jnp.where(first_half, partner, kept)
    velocity = uncond + guidance[0] * (cond - uncond)
    change = sigma_of(step_index[0] + 1) - sigma_of(step_index[0])
    next_latent = latent[0] + change * velocity
    return (velocity[None], next_latent[None])


def solution(mesh):
    placed = (
        P("cfg", "req", "tok", None),
        P("cfg", "req", "tok", None),
        P("cfg", "req"),
        P("cfg", "req", None, None),
        P("req", "tok", "cfg"),
        P("req"),
        P("req"),
        P(None, None, "tok"),
        P(None, None, "tok"),
        P(),
        P(),
        P(),
        P("tok", None),
        P(None, "tok"),
        P("tok", None),
        P(),
    )
    return jax.shard_map(
        local,
        mesh=mesh,
        in_specs=placed,
        out_specs=(P("req", "tok", "cfg"), P("req", "tok", "cfg")),
        check_vma=False,
    )
```

profile of v0, /device:TPU:1, one launch (start us, length us, event | category | flops | bytes accessed | tf_op | source)
XLA Modules:
  0.0 427.1 jit_solution(319573839320007998)
XLA Ops:
  7.2 1.2 slice_reduce_fusion.2
  8.5 1.0 convert_reduce_fusion.1
  9.5 1.1 fusion.48
  10.6 1.6 fusion.51
  12.3 1.1 convert_reduce_fusion
  13.4 1.2 fusion.34
  14.6 1.9 fusion.37
  16.7 3.9 copy.24
  20.6 2.5 copy.43
  23.1 2.5 copy.27
  26.2 36.2 %all-gather.6.cloned.1.call-done = bf16[256,2432]{1,0:T(8,128)(2,1)} async-done(((bf16[16,2432]{1,0:T(8,128)(2,1)}), bf16[256,2432]{1,0:T(8,128)(2,1)}) %all-gather.6.cloned.1.call-update) | async-done | bytes 1245200 | tf_op jit(solution)/shard_map/all_gather | solution.py:40
  62.4 2.2 fusion.24
  64.8 0.7 copy.39
  65.6 0.7 copy.37
  66.3 59.6 %all-gather.4.cloned.1.call-done = bf16[1024,2432]{1,0:T(8,128)(2,1)} async-done(((bf16[64,2432]{1,0:T(8,128)(2,1)}), bf16[1024,2432]{1,0:T(8,128)(2,1)}) %all-gather.4.cloned.1.call-update) | async-done | bytes 4980752 | tf_op jit(solution)/shard_map/all_gather | solution.py:40
  125.9 5.2 %fusion.13 = f32[1024,3,2,64]{0,3,2,1:T(8,128)S(1)} fusion(bf16[3,2,64,2432]{3,2,1,0:T(8,128)(2,1)} %bitcast.132, bf16[1024,2432]{1,0:T(8,128)(2,1)} %all-gather.4.cloned.1.call-done), kind=kOutput, calls=%fused_computation.17 | convolution fusion | flops 1912602624 | bytes 8421376 | tf_op jit(solution)/shard_map/dot_general | solution.py:82
  131.6 0.8 fusion.61
  132.6 1.1 copy.36
  133.8 1.6 pad_maximum_fusion.2
  135.3 1.6 pad_maximum_fusion.1
  136.9 25.1 %while.13 = (s32[]{:T(128)}, bf16[4,512,64]{1,2,0:T(8,128)(2,1)}, s32[4]{0:T(128)S(1)}, bf16[1024,128]{0,1:T(8,128)(2,1)}, bf16[1280,128]{1,0:T(8,128)(2,1)}, /*...) while((s32[]{:T(128)}, bf16[4,512,64]{1,2,0:T(8,128)(2,1)}, ...), condition=%wide.region_9.10_spmd.clone, body=%wide.region_7.9_spmd.clone.sunk | while | flops 171082528 | bytes 7349204 | solution.py:132
  136.9 0.6 dynamic_slice.60
  140.0 1.8 fusion.77
  141.9 1.3 fusion.78
  143.2 0.6 dynamic_slice.60
  146.3 1.8 fusion.77
  148.1 1.3 fusion.78
  149.5 0.6 dynamic_slice.60
  152.5 1.8 fusion.77
  154.4 1.3 fusion.78
  155.7 0.6 dynamic_slice.60
  158.8 1.8 fusion.77
  160.7 1.3 fusion.78
  162.0 1.2 copy.31
  163.4 4.8 %convolution_convert_fusion.1 = bf16[1024,2432]{1,0:T(8,128)(2,1)} fusion(bf16[1024,128]{0,1:T(8,128)(2,1)S(1)} %bitcast.131, bf16[128,2432]{1,0:T(8,128)(2,1)} %param.30), kind=kOutput, calls=%fused_computation.16 | convolution fusion | flops 640024576 | bytes 5865472 | tf_op jit(solution)/shard_map/dot_general | solution.py:140
  168.2 82.8 %reduce-scatter.3.cloned.1.call-done = bf16[64,2432]{1,0:T(8,128)(2,1)} async-done(((bf16[1024,2432]{1,0:T(8,128)(2,1)}), bf16[64,2432]{1,0:T(8,128)(2,1)}) %reduce-scatter.3.cloned.1.call-update) | async-done | bytes 311312 | tf_op jit(solution)/shard_map/reduce_scatter | solution.py:44
  251.0 1.2 fusion.38
  252.2 1.2 multiply_reduce_fusion.1
  253.5 1.9 add_convert_fusion.1
  255.4 0.2 reduce-scatter.5.cloned.1.call-start
  255.6 60.9 %all-gather.8.cloned.1.call-done = bf16[1024,2432]{1,0:T(8,128)(2,1)} async-done(((bf16[64,2432]{1,0:T(8,128)(2,1)}), bf16[1024,2432]{1,0:T(8,128)(2,1)}) %all-gather.8.cloned.1.call-update) | async-done | bytes 4980752 | tf_op jit(solution)/shard_map/all_gather | solution.py:40
  316.6 12.2 %convolution_convert_fusion = bf16[1024,2432]{1,0:T(8,128)(2,1)} fusion(bf16[608,2432]{1,0:T(8,128)(2,1)S(1)} %copy-done, bf16[1024,2432]{1,0:T(8,128)(2,1)} %all-gather.8.cloned.1.call-done, bf16[2432,608]{0,1:T(8,128)(2,1)} %param.31), kind=kOutput, calls=%fused_computation.15 | convolution fusion | flops 6064668672 | bytes 15876096 | tf_op jit(solution)/shard_map/dot_general | solution.py:146
  328.8 82.8 %reduce-scatter.5.cloned.1.call-done = bf16[64,2432]{1,0:T(8,128)(2,1)} async-done(((bf16[1024,2432]{1,0:T(8,128)(2,1)}), bf16[64,2432]{1,0:T(8,128)(2,1)}) %reduce-scatter.5.cloned.1.call-update) | async-done | bytes 311312 | tf_op jit(solution)/shard_map/reduce_scatter | solution.py:44
  411.6 1.3 fusion.59
  412.9 1.4 multiply_reduce_fusion
  414.3 1.6 fusion.39
  416.0 2.6 collective-permute-start
  419.9 0.6 fusion.53
  (59 shorter events, 1.3 us)
Async XLA Ops:
  7.2 309.4 %copy-start = (bf16[608,2432]{1,0:T(8,128)(2,1)S(1)}, bf16[608,2432]{1,0:T(8,128)(2,1)}, u32[]{:S(2)}) copy-start(bf16[608,2432]{1,0:T(8,128)(2,1)} %param.32) | copy-start | bytes 8871940
  7.2 55.2 %all-gather.6.cloned.1.call-start = ((), (), s32[]{:S(2)}) async-start(), calls=%async_computation.3 | async-start | bytes 1323008 | tf_op jit(solution)/shard_map/all_gather | solution.py:40
  12.2 113.7 %all-gather.4.cloned.1.call-start = ((), (), s32[]{:S(2)}) async-start(), calls=%async_computation.2 | async-start | bytes 5292032 | tf_op jit(solution)/shard_map/all_gather | solution.py:40
  16.6 234.4 %reduce-scatter.3.cloned.1.call-start = ((), (), s32[]{:S(2)}) async-start(), calls=%async_computation.4 | async-start | bytes 5292032 | tf_op jit(solution)/shard_map/reduce_scatter | solution.py:44
  25.5 39.2 %copy-start.4 = (f32[64]{0:T(128)S(1)}, f32[64]{0:T(128)}, u32[]{:S(2)}) copy-start(f32[64]{0:T(128)} %param.29) | copy-start | bytes 772
  125.9 5.4 %copy-start.5 = (f32[64]{0:T(128)S(1)}, f32[64]{0:T(128)}, u32[]{:S(2)}) copy-start(f32[64]{0:T(128)} %param.27) | copy-start | bytes 772
  125.9 5.5 %copy-start.6 = (f32[64]{0:T(128)S(1)}, f32[64]{0:T(128)}, u32[]{:S(2)}) copy-start(f32[64]{0:T(128)} %param.28) | copy-start | bytes 772
  136.9 4.9 %copy-start.2 = (bf16[1280,128]{1,0:T(8,128)(2,1)S(1)}, bf16[1280,128]{1,0:T(8,128)(2,1)}, u32[]{:S(2)}) copy-start(bf16[1280,128]{1,0:T(8,128)(2,1)} %get-tuple-element.233) | copy-start | bytes 983044 | tf_op jit(solution)/shard_map/while
  143.2 4.9 %copy-start.2 = (bf16[1280,128]{1,0:T(8,128)(2,1)S(1)}, bf16[1280,128]{1,0:T(8,128)(2,1)}, u32[]{:S(2)}) copy-start(bf16[1280,128]{1,0:T(8,128)(2,1)} %get-tuple-element.233) | copy-start | bytes 983044 | tf_op jit(solution)/shard_map/while
  149.4 4.9 %copy-start.2 = (bf16[1280,128]{1,0:T(8,128)(2,1)S(1)}, bf16[1280,128]{1,0:T(8,128)(2,1)}, u32[]{:S(2)}) copy-start(bf16[1280,128]{1,0:T(8,128)(2,1)} %get-tuple-element.233) | copy-start | bytes 983044 | tf_op jit(solution)/shard_map/while
  155.7 4.9 %copy-start.2 = (bf16[1280,128]{1,0:T(8,128)(2,1)S(1)}, bf16[1280,128]{1,0:T(8,128)(2,1)}, u32[]{:S(2)}) copy-start(bf16[1280,128]{1,0:T(8,128)(2,1)} %get-tuple-element.233) | copy-start | bytes 983044 | tf_op jit(solution)/shard_map/while
  168.2 82.9 %copy-start.1 = (bf16[1,1,64,2432]{3,2,1,0:T(8,128)(2,1)S(1)}, bf16[1,1,64,2432]{3,2,1,0:T(8,128)(2,1)}, u32[]{:S(2)}) copy-start(bf16[1,1,64,2432]{3,2,1,0:T(8,128)(2,1)} %param.18) | copy-start | bytes 933892
  168.2 148.4 %all-gather.8.cloned.1.call-start = ((), (), s32[]{:S(2)}) async-start(), calls=%async_computation.5 | async-start | bytes 5292032 | tf_op jit(solution)/shard_map/all_gather | solution.py:40
  255.4 156.2 %reduce-scatter.5.cloned.1.call-start = ((), (), s32[]{:S(2)}) async-start(), calls=%async_computation.6 | async-start | bytes 5292032 | tf_op jit(solution)/shard_map/reduce_scatter | solution.py:44
  328.8 91.2 %copy-start.3 = (f32[1,64,32]{1,2,0:T(8,128)S(1)}, f32[1,64,32]{1,2,0:T(8,128)}, u32[]{:S(2)}) copy-start(f32[1,64,32]{1,2,0:T(8,128)} %param.22) | copy-start | bytes 24580
  416.0 4.0 collective-permute-start
Sparse Core Ops, SparseCore 0:
  12.4 50.0 all-gather.5
  64.8 61.0 all-gather.3
  168.3 82.6 reduce-scatter.2
  255.5 61.0 all-gather.7
  328.9 82.6 reduce-scatter.4
where the time goes:
time: 428 us; the launch traced here: 427 us
  waiting for transfers between devices  322 us (75%)
  matrix products  38.7 us (9%)
  other arithmetic  20.6 us (5%)
  local copies, waits for them, and re-layouts  16.4 us (4%)
  between operations  16.1 us (4%)
  loops' own time  9.88 us (2%)
    reduce_scatter x2, waiting for transfers between devices, scatter_tokens(): lax.psum_scatter(term(jnp.int32(0), own_count * lax.axis_size('tok')).ast...  166 us
    all_gather x3, waiting for transfers between devices, gather_tokens(): lax.all_gather(local_rows, 'tok', axis=0, tiled=True)  157 us
    dot_general x1, matrix products, mlp_term(): return jnp.dot(hidden, down_weight, preferred_element_type=jnp.float32)  12.2 us
    another operation x1, loops' own time, local(): outputs = lax.map(one_task, lax.iota(jnp.int32, heads_local * blocks))  9.88 us
    unnamed x18, local copies, waits for them, and re-layouts  9.19 us
  transfers between devices with their start and end apart: 6, of which 5 were waited for; matrix products, arithmetic and copies ran while one was open for 4% of the time, Pallas kernels for 0%

commit v1 on v0

--- a/solution.py
+++ b/solution.py
@@ -7,6 +7,22 @@
 STEPS = 28
 epsilon = 1e-06
 shift_factor = 3.0
+
+
+def collect(x, axis, dim):
+    ways, here, step = (lax.axis_size(axis), lax.axis_index(axis), x.shape[dim])
+    dims = [n * ways if d == dim else n for d, n in enumerate(x.shape)]
+    full = lax.dynamic_update_slice_in_dim(jnp.zeros(dims, x.dtype), x, here * step, axis=dim)
+    going_up = going_down = x
+    for far in range(1, ways // 2 + 1):
+        going_up = lax.ppermute(going_up, axis, [(d, (d + 1) % ways) for d in range(ways)])
+        full = lax.dynamic_update_slice_in_dim(full, going_up, (here - far) % ways * step, axis=dim)
+        if 2 * far < ways:
+            going_down = lax.ppermute(going_down, axis, [(d, (d - 1) % ways) for d in range(ways)])
+            full = lax.dynamic_update_slice_in_dim(
+                full, going_down, (here + far) % ways * step, axis=dim
+            )
+    return full
 
 
 def swapped(value, axis, distance):
@@ -37,7 +53,7 @@
 
 
 def gather_tokens(local_rows, project):
-    return project(lax.all_gather(local_rows, "tok", axis=0, tiled=True), jnp.int32(0))
+    return project(collect(local_rows, "tok", 0), jnp.int32(0))
 
 
 def scatter_tokens(term, own_count):

time: 428 us -> 529 us (1.24); the launches traced: 427 us -> 519 us
  starting transfers between devices: 2.96 us -> 114 us
  waiting for transfers between devices: 322 us -> 256 us
  local copies, waits for them, and re-layouts: 16.4 us -> 60.9 us
    all_gather x3 -> x0, waiting for transfers between devices: 157 us -> none  [gather_tokens(): lax.all_gather(local_rows, 'tok', axis=0, tiled=True)]
    ppermute x0 -> x45, starting transfers between devices: none -> 111 us  [the longest x21 99 us: collect(): lax.ppermute(going_down, axis, [(d, (d - 1) % ways) for d in range(ways)])]
    ppermute x0 -> x45, waiting for transfers between devices: none -> 66.9 us  [the longest x24 66.3 us: collect(): lax.ppermute(going_up, axis, [(d, (d + 1) % ways) for d in range(ways)])]
    dynamic_update_slice x0 -> x45, local copies, waits for them, and re-layouts: none -> 35.9 us  [the longest x24 19 us: collect(): lax.dynamic_update_slice_in_dim(full, going_up, (here - far) % ways * ste...]
    reduce_scatter x2, waiting for transfers between devices: 166 us -> 189 us  [scatter_tokens(): lax.psum_scatter(term(jnp.int32(0), own_count * lax.axis_size('tok')).ast...]
    convert_element_type x3 -> x0, other arithmetic: 5.45 us -> none  [modulate(): (layer_norm(values) * (1.0 + shifts[scale_at]) + shifts[shift_at]).astype...]
  transfers between devices with their start and end apart: 6 -> 48, of which waited for: 5 -> 24; matrix products, arithmetic and copies ran while one was open for 4% -> 10% of each run, Pallas kernels for 0% -> 0%
where the time goes in v1:
time: 529 us; the launch traced here: 519 us
  waiting for transfers between devices  256 us (48%)
  starting transfers between devices  114 us (22%)
  local copies, waits for them, and re-layouts  60.9 us (12%)
  matrix products  41.9 us (8%)
  other arithmetic  20.2 us (4%)
  between operations  17.1 us (3%)
  loops' own time  9.11 us (2%)
    reduce_scatter x2, waiting for transfers between devices, scatter_tokens(): lax.psum_scatter(term(jnp.int32(0), own_count * lax.axis_size('tok')).ast...  189 us
    ppermute x21, starting transfers between devices, collect(): lax.ppermute(going_down, axis, [(d, (d - 1) % ways) for d in range(ways)])  99 us
    ppermute x24, waiting for transfers between devices, collect(): lax.ppermute(going_up, axis, [(d, (d + 1) % ways) for d in range(ways)])  66.3 us
    dynamic_update_slice x24, local copies, waits for them, and re-layouts, collect(): lax.dynamic_update_slice_in_dim(full, going_up, (here - far) % ways * ste...  19 us
    dynamic_update_slice x21, local copies, waits for them, and re-layouts, collect(): lax.dynamic_update_slice_in_dim(full, going_down, (here + far) % ways * s...  16.9 us
    ppermute x24, starting transfers between devices, collect(): lax.ppermute(going_up, axis, [(d, (d + 1) % ways) for d in range(ways)])  12.2 us
    dot_general x1, matrix products, mlp_term(): return jnp.dot(hidden, down_weight, preferred_element_type=jnp.float32)  12.1 us
  transfers between devices with their start and end apart: 48, of which 24 were waited for; matrix products, arithmetic and copies ran while one was open for 10% of the time, Pallas kernels for 0%

profile of v1, /device:TPU:1, one launch (start us, length us, event | category | flops | bytes accessed | tf_op | source)
XLA Modules:
  0.0 519.4 jit_solution(10677779375097655115)
XLA Ops:
  16.1 3.7 collective-permute-start.16
  22.7 2.5 broadcast.174.clone
  26.3 4.8 collective-permute-start.1
  31.1 2.5 copy.43
  33.6 2.4 copy.27
  36.0 3.9 copy.24
  40.9 4.8 collective-permute-start.18
  47.5 4.8 collective-permute-start.20
  54.0 4.8 collective-permute-start.22
  60.6 4.8 collective-permute-start.24
  65.7 4.8 collective-permute-start.3
  75.1 4.8 collective-permute-start.26
  82.9 4.8 collective-permute-start.28
  90.8 5.3 %collective-permute-done.29 = bf16[16,2432]{1,0:T(8,128)(2,1)S(1)} collective-permute-done((bf16[16,2432]{1,0:T(8,128)(2,1)S(1)}, bf16[16,2432]{1,0:T(8,128)(2,1)S(1)}, u32[]{:S(2)}, u32[]{:S(2)}) %collective-permute-start.29) | collective-permute-done | bytes 77856 | tf_op jit(solution)/shard_map/ppermute | solution.py:18
  100.6 4.8 collective-permute-start.5
  109.8 4.8 collective-permute-start.7
  116.1 4.2 collective-permute-done.6
  120.3 4.8 collective-permute-start.9
  126.6 3.3 collective-permute-done.8
  130.0 4.8 collective-permute-start.11
  136.2 2.8 collective-permute-done.10
  139.0 8.5 %collective-permute-start.12 = (bf16[64,2432]{1,0:T(8,128)(2,1)S(1)}, bf16[64,2432]{1,0:T(8,128)(2,1)S(1)}, u32[]{:S(2)}, u32[]{:S(2)}) collective-permute-start(bf16[64,2432]{1,0:T(8,128)(2,1)S(1)} %collective-permute-done.10), channel_id=1, source_target_pairs={{0,1},{1,2},{2,3},{3,4},{4,5},{5,6},{6,7},{7,8},{8,9},{9,10},{10,1... | collective-permute-start | bytes 933896 | tf_op jit(solution)/shard_map/ppermute | solution.py:18
  147.6 4.8 collective-permute-start.13
  153.8 2.8 collective-permute-done.12
  158.1 7.6 %collective-permute-done.14 = bf16[64,2432]{1,0:T(8,128)(2,1)S(1)} collective-permute-done((bf16[64,2432]{1,0:T(8,128)(2,1)S(1)}, bf16[64,2432]{1,0:T(8,128)(2,1)S(1)}, u32[]{:S(2)}, u32[]{:S(2)}) %collective-permute-start.14) | collective-permute-done | bytes 311328 | tf_op jit(solution)/shard_map/ppermute | solution.py:18
  166.5 4.7 fusion.13
  177.7 28.0 %while.13 = (s32[]{:T(128)}, bf16[4,512,64]{1,2,0:T(8,128)(2,1)}, s32[4]{0:T(128)S(1)}, bf16[1024,128]{0,1:T(8,128)(2,1)}, bf16[1280,128]{1,0:T(8,128)(2,1)}, /*...) while((s32[]{:T(128)}, bf16[4,512,64]{1,2,0:T(8,128)(2,1)}, ...), condition=%wide.region_9.10_spmd.clone, body=%wide.region_7.9_spmd.clone.sunk | while | flops 171082528 | bytes 6038456 | solution.py:148
  208.8 4.8 convolution_convert_fusion.1
  213.6 99.6 %reduce-scatter.3.cloned.1.call-done = bf16[64,2432]{1,0:T(8,128)(2,1)} async-done(((bf16[1024,2432]{1,0:T(8,128)(2,1)}), bf16[64,2432]{1,0:T(8,128)(2,1)}) %reduce-scatter.3.cloned.1.call-update) | async-done | bytes 311312 | tf_op jit(solution)/shard_map/reduce_scatter | solution.py:60
  315.8 2.6 broadcast.174
  320.3 3.8 collective-permute-start.31
  324.1 5.0 collective-permute-done.30
  329.8 4.8 collective-permute-start.33
  335.3 2.8 collective-permute-done.32
  339.1 4.8 collective-permute-start.35
  344.6 2.8 collective-permute-done.34
  348.2 4.8 collective-permute-start.37
  353.7 2.8 collective-permute-done.36
  357.2 4.8 collective-permute-start.39
  362.8 3.1 collective-permute-done.38
  366.7 5.1 collective-permute-start.41
  372.5 4.0 collective-permute-done.40
  377.3 5.2 %collective-permute-start.43 = (bf16[64,2432]{1,0:T(8,128)(2,1)S(1)}, bf16[64,2432]{1,0:T(8,128)(2,1)S(1)}, u32[]{:S(2)}, u32[]{:S(2)}) collective-permute-start(bf16[64,2432]{1,0:T(8,128)(2,1)S(1)} %collective-permute-done.41), channel_id=1, source_target_pairs={{0,15},{1,0},{2,1},{3,2},{4,3},{5,4},{6,5},{7,6},{8,7},{9,8},{10,9... | collective-permute-start | bytes 933896 | tf_op jit(solution)/shard_map/ppermute | solution.py:21
  383.3 4.9 collective-permute-done.42
  390.1 10.3 %collective-permute-done.44 = bf16[64,2432]{1,0:T(8,128)(2,1)S(1)} collective-permute-done((bf16[64,2432]{1,0:T(8,128)(2,1)S(1)}, bf16[64,2432]{1,0:T(8,128)(2,1)S(1)}, u32[]{:S(2)}, u32[]{:S(2)}) %collective-permute-start.44) | collective-permute-done | bytes 311328 | tf_op jit(solution)/shard_map/ppermute | solution.py:18
  401.1 12.1 %convolution_convert_fusion = bf16[1024,2432]{1,0:T(8,128)(2,1)} fusion(bf16[608,2432]{1,0:T(8,128)(2,1)S(1)} %copy-done, bf16[1024,2432]{1,0:T(8,128)(2,1)} %constant_dynamic-update-slice_fusion, bf16[2432,608]{0,1:T(8,128)(2,1)} %param.31), kind=kOutput, calls=%fused_computation.15 | convolution fusion | flops 6064668672 | bytes 15876096 | tf_op jit(solution)/shard_map/dot_general | solution.py:162
  413.3 89.8 %reduce-scatter.5.cloned.1.call-done = bf16[64,2432]{1,0:T(8,128)(2,1)} async-done(((bf16[1024,2432]{1,0:T(8,128)(2,1)}), bf16[64,2432]{1,0:T(8,128)(2,1)}) %reduce-scatter.5.cloned.1.call-update) | async-done | bytes 311312 | tf_op jit(solution)/shard_map/reduce_scatter | solution.py:60
  507.5 2.6 collective-permute-start.45
  (194 shorter events, 96.4 us)
Async XLA Ops:
  7.2 306.1 %reduce-scatter.3.cloned.1.call-start = ((), (), s32[]{:S(2)}) async-start(), calls=%async_computation.2 | async-start | bytes 5292032 | tf_op jit(solution)/shard_map/reduce_scatter | solution.py:60
  14.0 26.8 %collective-permute-start.15 = (bf16[16,2432]{1,0:T(8,128)(2,1)S(1)}, bf16[16,2432]{1,0:T(8,128)(2,1)S(1)}, u32[]{:S(2)}, u32[]{:S(2)}) collective-permute-start(bf16[16,2432]{1,0:T(8,128)(2,1)S(1)} %get-tuple-element.141), channel_id=1, source_target_pairs={{0,1},{1,2},{2,3},{3,4},{4,5},{5,6},{6,7},{7,8},{8,9},{9,10},{10,1... | collective-permute-start | bytes 233480 | tf_op jit(solution)/shard_map/ppermute | solution.py:18
  16.1 24.8 %collective-permute-start.16 = (bf16[16,2432]{1,0:T(8,128)(2,1)S(1)}, bf16[16,2432]{1,0:T(8,128)(2,1)S(1)}, u32[]{:S(2)}, u32[]{:S(2)}) collective-permute-start(bf16[16,2432]{1,0:T(8,128)(2,1)S(1)} %get-tuple-element.141), channel_id=1, source_target_pairs={{0,15},{1,0},{2,1},{3,2},{4,3},{5,4},{6,5},{7,6},{8,7},{9,8},{10,9... | collective-permute-start | bytes 233480 | tf_op jit(solution)/shard_map/ppermute | solution.py:21
  26.3 39.1 %collective-permute-start = (bf16[64,2432]{1,0:T(8,128)(2,1)}, bf16[64,2432]{1,0:T(8,128)(2,1)}, u32[]{:S(2)}, u32[]{:S(2)}) collective-permute-start(bf16[64,2432]{1,0:T(8,128)(2,1)} %get-tuple-element.143), channel_id=1, source_target_pairs={{0,1},{1,2},{2,3},{3,4},{4,5},{5,6},{6,7},{7,8},{8,9},{9,10},{10,1... | collective-permute-start | bytes 933896 | tf_op jit(solution)/shard_map/ppermute | solution.py:18
  26.3 39.3 %collective-permute-start.1 = (bf16[64,2432]{1,0:T(8,128)(2,1)}, bf16[64,2432]{1,0:T(8,128)(2,1)}, u32[]{:S(2)}, u32[]{:S(2)}) collective-permute-start(bf16[64,2432]{1,0:T(8,128)(2,1)} %get-tuple-element.143), channel_id=1, source_target_pairs={{0,15},{1,0},{2,1},{3,2},{4,3},{5,4},{6,5},{7,6},{8,7},{9,8},{10,9... | collective-permute-start | bytes 933896 | tf_op jit(solution)/shard_map/ppermute | solution.py:21
  40.8 6.6 %collective-permute-start.17 = (bf16[16,2432]{1,0:T(8,128)(2,1)S(1)}, bf16[16,2432]{1,0:T(8,128)(2,1)S(1)}, u32[]{:S(2)}, u32[]{:S(2)}) collective-permute-start(bf16[16,2432]{1,0:T(8,128)(2,1)S(1)} %collective-permute-done.15), channel_id=1, source_target_pairs={{0,1},{1,2},{2,3},{3,4},{4,5},{5,6},{6,7},{7,8},{8,9},{9,10},{10,1... | collective-permute-start | bytes 233480 | tf_op jit(solution)/shard_map/ppermute | solution.py:18
  40.9 6.5 %collective-permute-start.18 = (bf16[16,2432]{1,0:T(8,128)(2,1)S(1)}, bf16[16,2432]{1,0:T(8,128)(2,1)S(1)}, u32[]{:S(2)}, u32[]{:S(2)}) collective-permute-start(bf16[16,2432]{1,0:T(8,128)(2,1)S(1)} %collective-permute-done.16), channel_id=1, source_target_pairs={{0,15},{1,0},{2,1},{3,2},{4,3},{5,4},{6,5},{7,6},{8,7},{9,8},{10,9... | collective-permute-start | bytes 233480 | tf_op jit(solution)/shard_map/ppermute | solution.py:21
  47.5 6.6 %collective-permute-start.19 = (bf16[16,2432]{1,0:T(8,128)(2,1)S(1)}, bf16[16,2432]{1,0:T(8,128)(2,1)S(1)}, u32[]{:S(2)}, u32[]{:S(2)}) collective-permute-start(bf16[16,2432]{1,0:T(8,128)(2,1)S(1)} %collective-permute-done.17), channel_id=1, source_target_pairs={{0,1},{1,2},{2,3},{3,4},{4,5},{5,6},{6,7},{7,8},{8,9},{9,10},{10,1... | collective-permute-start | bytes 233480 | tf_op jit(solution)/shard_map/ppermute | solution.py:18
  47.5 6.6 %collective-permute-start.20 = (bf16[16,2432]{1,0:T(8,128)(2,1)S(1)}, bf16[16,2432]{1,0:T(8,128)(2,1)S(1)}, u32[]{:S(2)}, u32[]{:S(2)}) collective-permute-start(bf16[16,2432]{1,0:T(8,128)(2,1)S(1)} %collective-permute-done.18), channel_id=1, source_target_pairs={{0,15},{1,0},{2,1},{3,2},{4,3},{5,4},{6,5},{7,6},{8,7},{9,8},{10,9... | collective-permute-start | bytes 233480 | tf_op jit(solution)/shard_map/ppermute | solution.py:21
  54.0 6.6 %collective-permute-start.21 = (bf16[16,2432]{1,0:T(8,128)(2,1)S(1)}, bf16[16,2432]{1,0:T(8,128)(2,1)S(1)}, u32[]{:S(2)}, u32[]{:S(2)}) collective-permute-start(bf16[16,2432]{1,0:T(8,128)(2,1)S(1)} %collective-permute-done.19), channel_id=1, source_target_pairs={{0,1},{1,2},{2,3},{3,4},{4,5},{5,6},{6,7},{7,8},{8,9},{9,10},{10,1... | collective-permute-start | bytes 233480 | tf_op jit(solution)/shard_map/ppermute | solution.py:18
  54.0 6.6 %collective-permute-start.22 = (bf16[16,2432]{1,0:T(8,128)(2,1)S(1)}, bf16[16,2432]{1,0:T(8,128)(2,1)S(1)}, u32[]{:S(2)}, u32[]{:S(2)}) collective-permute-start(bf16[16,2432]{1,0:T(8,128)(2,1)S(1)} %collective-permute-done.20), channel_id=1, source_target_pairs={{0,15},{1,0},{2,1},{3,2},{4,3},{5,4},{6,5},{7,6},{8,7},{9,8},{10,9... | collective-permute-start | bytes 233480 | tf_op jit(solution)/shard_map/ppermute | solution.py:21
  60.6 14.5 %collective-permute-start.23 = (bf16[16,2432]{1,0:T(8,128)(2,1)S(1)}, bf16[16,2432]{1,0:T(8,128)(2,1)S(1)}, u32[]{:S(2)}, u32[]{:S(2)}) collective-permute-start(bf16[16,2432]{1,0:T(8,128)(2,1)S(1)} %collective-permute-done.21), channel_id=1, source_target_pairs={{0,1},{1,2},{2,3},{3,4},{4,5},{5,6},{6,7},{7,8},{8,9},{9,10},{10,1... | collective-permute-start | bytes 233480 | tf_op jit(solution)/shard_map/ppermute | solution.py:18
  60.6 14.5 %collective-permute-start.24 = (bf16[16,2432]{1,0:T(8,128)(2,1)S(1)}, bf16[16,2432]{1,0:T(8,128)(2,1)S(1)}, u32[]{:S(2)}, u32[]{:S(2)}) collective-permute-start(bf16[16,2432]{1,0:T(8,128)(2,1)S(1)} %collective-permute-done.22), channel_id=1, source_target_pairs={{0,15},{1,0},{2,1},{3,2},{4,3},{5,4},{6,5},{7,6},{8,7},{9,8},{10,9... | collective-permute-start | bytes 233480 | tf_op jit(solution)/shard_map/ppermute | solution.py:21
  65.4 35.1 %collective-permute-start.2 = (bf16[64,2432]{1,0:T(8,128)(2,1)}, bf16[64,2432]{1,0:T(8,128)(2,1)}, u32[]{:S(2)}, u32[]{:S(2)}) collective-permute-start(bf16[64,2432]{1,0:T(8,128)(2,1)} %collective-permute-done), channel_id=1, source_target_pairs={{0,1},{1,2},{2,3},{3,4},{4,5},{5,6},{6,7},{7,8},{8,9},{9,10},{10,1... | collective-permute-start | bytes 933896 | tf_op jit(solution)/shard_map/ppermute | solution.py:18
  65.7 34.9 %collective-permute-start.3 = (bf16[64,2432]{1,0:T(8,128)(2,1)}, bf16[64,2432]{1,0:T(8,128)(2,1)}, u32[]{:S(2)}, u32[]{:S(2)}) collective-permute-start(bf16[64,2432]{1,0:T(8,128)(2,1)} %collective-permute-done.1), channel_id=1, source_target_pairs={{0,15},{1,0},{2,1},{3,2},{4,3},{5,4},{6,5},{7,6},{8,7},{9,8},{10,9... | collective-permute-start | bytes 933896 | tf_op jit(solution)/shard_map/ppermute | solution.py:21
  75.1 7.8 %collective-permute-start.25 = (bf16[16,2432]{1,0:T(8,128)(2,1)S(1)}, bf16[16,2432]{1,0:T(8,128)(2,1)S(1)}, u32[]{:S(2)}, u32[]{:S(2)}) collective-permute-start(bf16[16,2432]{1,0:T(8,128)(2,1)S(1)} %collective-permute-done.23), channel_id=1, source_target_pairs={{0,1},{1,2},{2,3},{3,4},{4,5},{5,6},{6,7},{7,8},{8,9},{9,10},{10,1... | collective-permute-start | bytes 233480 | tf_op jit(solution)/shard_map/ppermute | solution.py:18
  75.1 7.8 %collective-permute-start.26 = (bf16[16,2432]{1,0:T(8,128)(2,1)S(1)}, bf16[16,2432]{1,0:T(8,128)(2,1)S(1)}, u32[]{:S(2)}, u32[]{:S(2)}) collective-permute-start(bf16[16,2432]{1,0:T(8,128)(2,1)S(1)} %collective-permute-done.24), channel_id=1, source_target_pairs={{0,15},{1,0},{2,1},{3,2},{4,3},{5,4},{6,5},{7,6},{8,7},{9,8},{10,9... | collective-permute-start | bytes 233480 | tf_op jit(solution)/shard_map/ppermute | solution.py:21
  82.9 6.6 %collective-permute-start.27 = (bf16[16,2432]{1,0:T(8,128)(2,1)S(1)}, bf16[16,2432]{1,0:T(8,128)(2,1)S(1)}, u32[]{:S(2)}, u32[]{:S(2)}) collective-permute-start(bf16[16,2432]{1,0:T(8,128)(2,1)S(1)} %collective-permute-done.25), channel_id=1, source_target_pairs={{0,1},{1,2},{2,3},{3,4},{4,5},{5,6},{6,7},{7,8},{8,9},{9,10},{10,1... | collective-permute-start | bytes 233480 | tf_op jit(solution)/shard_map/ppermute | solution.py:18
  82.9 7.2 %collective-permute-start.28 = (bf16[16,2432]{1,0:T(8,128)(2,1)S(1)}, bf16[16,2432]{1,0:T(8,128)(2,1)S(1)}, u32[]{:S(2)}, u32[]{:S(2)}) collective-permute-start(bf16[16,2432]{1,0:T(8,128)(2,1)S(1)} %collective-permute-done.26), channel_id=1, source_target_pairs={{0,15},{1,0},{2,1},{3,2},{4,3},{5,4},{6,5},{7,6},{8,7},{9,8},{10,9... | collective-permute-start | bytes 233480 | tf_op jit(solution)/shard_map/ppermute | solution.py:21
  89.5 6.6 %collective-permute-start.29 = (bf16[16,2432]{1,0:T(8,128)(2,1)S(1)}, bf16[16,2432]{1,0:T(8,128)(2,1)S(1)}, u32[]{:S(2)}, u32[]{:S(2)}) collective-permute-start(bf16[16,2432]{1,0:T(8,128)(2,1)S(1)} %collective-permute-done.27), channel_id=1, source_target_pairs={{0,1},{1,2},{2,3},{3,4},{4,5},{5,6},{6,7},{7,8},{8,9},{9,10},{10,1... | collective-permute-start | bytes 233480 | tf_op jit(solution)/shard_map/ppermute | solution.py:18
  100.5 9.3 %collective-permute-start.4 = (bf16[64,2432]{1,0:T(8,128)(2,1)}, bf16[64,2432]{1,0:T(8,128)(2,1)S(1)}, u32[]{:S(2)}, u32[]{:S(2)}) collective-permute-start(bf16[64,2432]{1,0:T(8,128)(2,1)} %collective-permute-done.2), channel_id=1, source_target_pairs={{0,1},{1,2},{2,3},{3,4},{4,5},{5,6},{6,7},{7,8},{8,9},{9,10},{10,1... | collective-permute-start | bytes 933896 | tf_op jit(solution)/shard_map/ppermute | solution.py:18
  100.6 9.3 %collective-permute-start.5 = (bf16[64,2432]{1,0:T(8,128)(2,1)}, bf16[64,2432]{1,0:T(8,128)(2,1)S(1)}, u32[]{:S(2)}, u32[]{:S(2)}) collective-permute-start(bf16[64,2432]{1,0:T(8,128)(2,1)} %collective-permute-done.3), channel_id=1, source_target_pairs={{0,15},{1,0},{2,1},{3,2},{4,3},{5,4},{6,5},{7,6},{8,7},{9,8},{10,9... | collective-permute-start | bytes 933896 | tf_op jit(solution)/shard_map/ppermute | solution.py:21
  109.8 10.5 %collective-permute-start.6 = (bf16[64,2432]{1,0:T(8,128)(2,1)S(1)}, bf16[64,2432]{1,0:T(8,128)(2,1)S(1)}, u32[]{:S(2)}, u32[]{:S(2)}) collective-permute-start(bf16[64,2432]{1,0:T(8,128)(2,1)S(1)} %collective-permute-done.4), channel_id=1, source_target_pairs={{0,1},{1,2},{2,3},{3,4},{4,5},{5,6},{6,7},{7,8},{8,9},{9,10},{10,1... | collective-permute-start | bytes 933896 | tf_op jit(solution)/shard_map/ppermute | solution.py:18
  109.8 10.5 %collective-permute-start.7 = (bf16[64,2432]{1,0:T(8,128)(2,1)S(1)}, bf16[64,2432]{1,0:T(8,128)(2,1)S(1)}, u32[]{:S(2)}, u32[]{:S(2)}) collective-permute-start(bf16[64,2432]{1,0:T(8,128)(2,1)S(1)} %collective-permute-done.5), channel_id=1, source_target_pairs={{0,15},{1,0},{2,1},{3,2},{4,3},{5,4},{6,5},{7,6},{8,7},{9,8},{10,9... | collective-permute-start | bytes 933896 | tf_op jit(solution)/shard_map/ppermute | solution.py:21
  120.3 9.6 %collective-permute-start.8 = (bf16[64,2432]{1,0:T(8,128)(2,1)S(1)}, bf16[64,2432]{1,0:T(8,128)(2,1)S(1)}, u32[]{:S(2)}, u32[]{:S(2)}) collective-permute-start(bf16[64,2432]{1,0:T(8,128)(2,1)S(1)} %collective-permute-done.6), channel_id=1, source_target_pairs={{0,1},{1,2},{2,3},{3,4},{4,5},{5,6},{6,7},{7,8},{8,9},{9,10},{10,1... | collective-permute-start | bytes 933896 | tf_op jit(solution)/shard_map/ppermute | solution.py:18
  120.3 9.6 %collective-permute-start.9 = (bf16[64,2432]{1,0:T(8,128)(2,1)S(1)}, bf16[64,2432]{1,0:T(8,128)(2,1)S(1)}, u32[]{:S(2)}, u32[]{:S(2)}) collective-permute-start(bf16[64,2432]{1,0:T(8,128)(2,1)S(1)} %collective-permute-done.7), channel_id=1, source_target_pairs={{0,15},{1,0},{2,1},{3,2},{4,3},{5,4},{6,5},{7,6},{8,7},{9,8},{10,9... | collective-permute-start | bytes 933896 | tf_op jit(solution)/shard_map/ppermute | solution.py:21
  129.9 9.1 %collective-permute-start.10 = (bf16[64,2432]{1,0:T(8,128)(2,1)S(1)}, bf16[64,2432]{1,0:T(8,128)(2,1)S(1)}, u32[]{:S(2)}, u32[]{:S(2)}) collective-permute-start(bf16[64,2432]{1,0:T(8,128)(2,1)S(1)} %collective-permute-done.8), channel_id=1, source_target_pairs={{0,1},{1,2},{2,3},{3,4},{4,5},{5,6},{6,7},{7,8},{8,9},{9,10},{10,1... | collective-permute-start | bytes 933896 | tf_op jit(solution)/shard_map/ppermute | solution.py:18
  130.0 17.6 %collective-permute-start.11 = (bf16[64,2432]{1,0:T(8,128)(2,1)S(1)}, bf16[64,2432]{1,0:T(8,128)(2,1)S(1)}, u32[]{:S(2)}, u32[]{:S(2)}) collective-permute-start(bf16[64,2432]{1,0:T(8,128)(2,1)S(1)} %collective-permute-done.9), channel_id=1, source_target_pairs={{0,15},{1,0},{2,1},{3,2},{4,3},{5,4},{6,5},{7,6},{8,7},{9,8},{10,9... | collective-permute-start | bytes 933896 | tf_op jit(solution)/shard_map/ppermute | solution.py:21
  139.0 17.6 %collective-permute-start.12 = (bf16[64,2432]{1,0:T(8,128)(2,1)S(1)}, bf16[64,2432]{1,0:T(8,128)(2,1)S(1)}, u32[]{:S(2)}, u32[]{:S(2)}) collective-permute-start(bf16[64,2432]{1,0:T(8,128)(2,1)S(1)} %collective-permute-done.10), channel_id=1, source_target_pairs={{0,1},{1,2},{2,3},{3,4},{4,5},{5,6},{6,7},{7,8},{8,9},{9,10},{10,1... | collective-permute-start | bytes 933896 | tf_op jit(solution)/shard_map/ppermute | solution.py:18
  147.6 9.8 %collective-permute-start.13 = (bf16[64,2432]{1,0:T(8,128)(2,1)S(1)}, bf16[64,2432]{1,0:T(8,128)(2,1)S(1)}, u32[]{:S(2)}, u32[]{:S(2)}) collective-permute-start(bf16[64,2432]{1,0:T(8,128)(2,1)S(1)} %collective-permute-done.11), channel_id=1, source_target_pairs={{0,15},{1,0},{2,1},{3,2},{4,3},{5,4},{6,5},{7,6},{8,7},{9,8},{10,9... | collective-permute-start | bytes 933896 | tf_op jit(solution)/shard_map/ppermute | solution.py:21
  156.6 9.1 %collective-permute-start.14 = (bf16[64,2432]{1,0:T(8,128)(2,1)S(1)}, bf16[64,2432]{1,0:T(8,128)(2,1)S(1)}, u32[]{:S(2)}, u32[]{:S(2)}) collective-permute-start(bf16[64,2432]{1,0:T(8,128)(2,1)S(1)} %collective-permute-done.12), channel_id=1, source_target_pairs={{0,1},{1,2},{2,3},{3,4},{4,5},{5,6},{6,7},{7,8},{8,9},{9,10},{10,1... | collective-permute-start | bytes 933896 | tf_op jit(solution)/shard_map/ppermute | solution.py:18
  213.6 289.5 %reduce-scatter.5.cloned.1.call-start = ((), (), s32[]{:S(2)}) async-start(), calls=%async_computation.3 | async-start | bytes 5292032 | tf_op jit(solution)/shard_map/reduce_scatter | solution.py:60
  319.3 9.8 %collective-permute-start.30 = (bf16[64,2432]{1,0:T(8,128)(2,1)S(1)}, bf16[64,2432]{1,0:T(8,128)(2,1)S(1)}, u32[]{:S(2)}, u32[]{:S(2)}) collective-permute-start(bf16[64,2432]{1,0:T(8,128)(2,1)S(1)} %get-tuple-element.139), channel_id=1, source_target_pairs={{0,1},{1,2},{2,3},{3,4},{4,5},{5,6},{6,7},{7,8},{8,9},{9,10},{10,1... | collective-permute-start | bytes 933896 | tf_op jit(solution)/shard_map/ppermute | solution.py:18
  320.3 9.5 %collective-permute-start.31 = (bf16[64,2432]{1,0:T(8,128)(2,1)S(1)}, bf16[64,2432]{1,0:T(8,128)(2,1)S(1)}, u32[]{:S(2)}, u32[]{:S(2)}) collective-permute-start(bf16[64,2432]{1,0:T(8,128)(2,1)S(1)} %get-tuple-element.139), channel_id=1, source_target_pairs={{0,15},{1,0},{2,1},{3,2},{4,3},{5,4},{6,5},{7,6},{8,7},{9,8},{10,9... | collective-permute-start | bytes 933896 | tf_op jit(solution)/shard_map/ppermute | solution.py:21
  329.1 9.1 %collective-permute-start.32 = (bf16[64,2432]{1,0:T(8,128)(2,1)S(1)}, bf16[64,2432]{1,0:T(8,128)(2,1)S(1)}, u32[]{:S(2)}, u32[]{:S(2)}) collective-permute-start(bf16[64,2432]{1,0:T(8,128)(2,1)S(1)} %collective-permute-done.30), channel_id=1, source_target_pairs={{0,1},{1,2},{2,3},{3,4},{4,5},{5,6},{6,7},{7,8},{8,9},{9,10},{10,1... | collective-permute-start | bytes 933896 | tf_op jit(solution)/shard_map/ppermute | solution.py:18
  329.8 9.3 %collective-permute-start.33 = (bf16[64,2432]{1,0:T(8,128)(2,1)S(1)}, bf16[64,2432]{1,0:T(8,128)(2,1)S(1)}, u32[]{:S(2)}, u32[]{:S(2)}) collective-permute-start(bf16[64,2432]{1,0:T(8,128)(2,1)S(1)} %collective-permute-done.31), channel_id=1, source_target_pairs={{0,15},{1,0},{2,1},{3,2},{4,3},{5,4},{6,5},{7,6},{8,7},{9,8},{10,9... | collective-permute-start | bytes 933896 | tf_op jit(solution)/shard_map/ppermute | solution.py:21
  338.1 9.3 %collective-permute-start.34 = (bf16[64,2432]{1,0:T(8,128)(2,1)S(1)}, bf16[64,2432]{1,0:T(8,128)(2,1)S(1)}, u32[]{:S(2)}, u32[]{:S(2)}) collective-permute-start(bf16[64,2432]{1,0:T(8,128)(2,1)S(1)} %collective-permute-done.32), channel_id=1, source_target_pairs={{0,1},{1,2},{2,3},{3,4},{4,5},{5,6},{6,7},{7,8},{8,9},{9,10},{10,1... | collective-permute-start | bytes 933896 | tf_op jit(solution)/shard_map/ppermute | solution.py:18
  339.1 9.1 %collective-permute-start.35 = (bf16[64,2432]{1,0:T(8,128)(2,1)S(1)}, bf16[64,2432]{1,0:T(8,128)(2,1)S(1)}, u32[]{:S(2)}, u32[]{:S(2)}) collective-permute-start(bf16[64,2432]{1,0:T(8,128)(2,1)S(1)} %collective-permute-done.33), channel_id=1, source_target_pairs={{0,15},{1,0},{2,1},{3,2},{4,3},{5,4},{6,5},{7,6},{8,7},{9,8},{10,9... | collective-permute-start | bytes 933896 | tf_op jit(solution)/shard_map/ppermute | solution.py:21
  347.4 9.1 %collective-permute-start.36 = (bf16[64,2432]{1,0:T(8,128)(2,1)S(1)}, bf16[64,2432]{1,0:T(8,128)(2,1)S(1)}, u32[]{:S(2)}, u32[]{:S(2)}) collective-permute-start(bf16[64,2432]{1,0:T(8,128)(2,1)S(1)} %collective-permute-done.34), channel_id=1, source_target_pairs={{0,1},{1,2},{2,3},{3,4},{4,5},{5,6},{6,7},{7,8},{8,9},{9,10},{10,1... | collective-permute-start | bytes 933896 | tf_op jit(solution)/shard_map/ppermute | solution.py:18
  348.2 9.1 %collective-permute-start.37 = (bf16[64,2432]{1,0:T(8,128)(2,1)S(1)}, bf16[64,2432]{1,0:T(8,128)(2,1)S(1)}, u32[]{:S(2)}, u32[]{:S(2)}) collective-permute-start(bf16[64,2432]{1,0:T(8,128)(2,1)S(1)} %collective-permute-done.35), channel_id=1, source_target_pairs={{0,15},{1,0},{2,1},{3,2},{4,3},{5,4},{6,5},{7,6},{8,7},{9,8},{10,9... | collective-permute-start | bytes 933896 | tf_op jit(solution)/shard_map/ppermute | solution.py:21
  356.5 9.4 %collective-permute-start.38 = (bf16[64,2432]{1,0:T(8,128)(2,1)S(1)}, bf16[64,2432]{1,0:T(8,128)(2,1)S(1)}, u32[]{:S(2)}, u32[]{:S(2)}) collective-permute-start(bf16[64,2432]{1,0:T(8,128)(2,1)S(1)} %collective-permute-done.36), channel_id=1, source_target_pairs={{0,1},{1,2},{2,3},{3,4},{4,5},{5,6},{6,7},{7,8},{8,9},{9,10},{10,1... | collective-permute-start | bytes 933896 | tf_op jit(solution)/shard_map/ppermute | solution.py:18
  357.2 9.4 %collective-permute-start.39 = (bf16[64,2432]{1,0:T(8,128)(2,1)S(1)}, bf16[64,2432]{1,0:T(8,128)(2,1)S(1)}, u32[]{:S(2)}, u32[]{:S(2)}) collective-permute-start(bf16[64,2432]{1,0:T(8,128)(2,1)S(1)} %collective-permute-done.37), channel_id=1, source_target_pairs={{0,15},{1,0},{2,1},{3,2},{4,3},{5,4},{6,5},{7,6},{8,7},{9,8},{10,9... | collective-permute-start | bytes 933896 | tf_op jit(solution)/shard_map/ppermute | solution.py:21
  365.9 10.6 %collective-permute-start.40 = (bf16[64,2432]{1,0:T(8,128)(2,1)S(1)}, bf16[64,2432]{1,0:T(8,128)(2,1)S(1)}, u32[]{:S(2)}, u32[]{:S(2)}) collective-permute-start(bf16[64,2432]{1,0:T(8,128)(2,1)S(1)} %collective-permute-done.38), channel_id=1, source_target_pairs={{0,1},{1,2},{2,3},{3,4},{4,5},{5,6},{6,7},{7,8},{8,9},{9,10},{10,1... | collective-permute-start | bytes 933896 | tf_op jit(solution)/shard_map/ppermute | solution.py:18
  366.7 10.7 %collective-permute-start.41 = (bf16[64,2432]{1,0:T(8,128)(2,1)S(1)}, bf16[64,2432]{1,0:T(8,128)(2,1)S(1)}, u32[]{:S(2)}, u32[]{:S(2)}) collective-permute-start(bf16[64,2432]{1,0:T(8,128)(2,1)S(1)} %collective-permute-done.39), channel_id=1, source_target_pairs={{0,15},{1,0},{2,1},{3,2},{4,3},{5,4},{6,5},{7,6},{8,7},{9,8},{10,9... | collective-permute-start | bytes 933896 | tf_op jit(solution)/shard_map/ppermute | solution.py:21
  376.5 11.7 %collective-permute-start.42 = (bf16[64,2432]{1,0:T(8,128)(2,1)S(1)}, bf16[64,2432]{1,0:T(8,128)(2,1)S(1)}, u32[]{:S(2)}, u32[]{:S(2)}) collective-permute-start(bf16[64,2432]{1,0:T(8,128)(2,1)S(1)} %collective-permute-done.40), channel_id=1, source_target_pairs={{0,1},{1,2},{2,3},{3,4},{4,5},{5,6},{6,7},{7,8},{8,9},{9,10},{10,1... | collective-permute-start | bytes 933896 | tf_op jit(solution)/shard_map/ppermute | solution.py:18
  377.3 12.0 %collective-permute-start.43 = (bf16[64,2432]{1,0:T(8,128)(2,1)S(1)}, bf16[64,2432]{1,0:T(8,128)(2,1)S(1)}, u32[]{:S(2)}, u32[]{:S(2)}) collective-permute-start(bf16[64,2432]{1,0:T(8,128)(2,1)S(1)} %collective-permute-done.41), channel_id=1, source_target_pairs={{0,15},{1,0},{2,1},{3,2},{4,3},{5,4},{6,5},{7,6},{8,7},{9,8},{10,9... | collective-permute-start | bytes 933896 | tf_op jit(solution)/shard_map/ppermute | solution.py:21
  388.2 12.2 %collective-permute-start.44 = (bf16[64,2432]{1,0:T(8,128)(2,1)S(1)}, bf16[64,2432]{1,0:T(8,128)(2,1)S(1)}, u32[]{:S(2)}, u32[]{:S(2)}) collective-permute-start(bf16[64,2432]{1,0:T(8,128)(2,1)S(1)} %collective-permute-done.42), channel_id=1, source_target_pairs={{0,1},{1,2},{2,3},{3,4},{4,5},{5,6},{6,7},{7,8},{8,9},{9,10},{10,1... | collective-permute-start | bytes 933896 | tf_op jit(solution)/shard_map/ppermute | solution.py:18
  507.5 4.0 collective-permute-start.45
  (13 other events, 1051.4 us)
Sparse Core Ops, SparseCore 0:
  213.7 99.4 reduce-scatter.2
  413.4 89.6 reduce-scatter.4
